TPU v7x, 32 devices: a whole 2x2x4 slice. The times are simulated.
32 devices in a mesh: parts: 2 (over x), grid: 8 (over z, y), depth: 2 (over core).
Axes of the slice: x: 2, y: 2, z: 4, core: 2. Of those that a mesh axis runs over, the one named last changes fastest.
Arguments:
- gate_input: bfloat16 [1024, 32768], P(('parts', 'depth'), 'grid'), parts along dimension 0, may hold values from -6 to 6
- up_input: bfloat16 [1024, 32768], P(('parts', 'depth'), 'grid'), parts along dimension 0, may hold values from -6 to 6
- code_values: bfloat16 [32768, 8192], P('grid', 'depth'), may hold values from -6 to 6, as said below
- exponents: int32 [1024, 8192], P('grid', 'depth'), may hold values from -10 to -7
- cotangent: bfloat16 [1024, 8192], P(('parts', 'depth'), 'grid'), parts along dimension 0, may hold values from -1.5 to 1.5
Outputs:
- output_rows: bfloat16 [1024, 8192], P(('parts', 'depth'), 'grid'), parts along dimension 0
- grad_gate: bfloat16 [1024, 32768], P(('parts', 'depth'), 'grid'), parts along dimension 0
- grad_up: bfloat16 [1024, 32768], P(('parts', 'depth'), 'grid'), parts along dimension 0
- grad_weight: bfloat16 [65536, 8192], P(('parts', 'grid'), 'depth'), parts along dimension 0
There are 2 independent parts, one for each index of `parts`. A program takes and returns all parts, laid end to end along the dimension named above; an argument that names none is the same for every part. Nothing has to cross between parts.
Inputs may be any that keep to these rules, and one draw needn't show every extreme that they name: `code_values`: every entry is one of the E2M1 values 0, +-0.5, +-1, +-1.5, +-2, +-3, +-4, +-6.
All inputs are finite; a program needn't handle non-finite values.
Results may differ from a plain program's by a relative error of at most 0.0049.
Values may be sent and summed in bfloat16 or wider, within the bound.
A program may use at most 448 MiB of HBM per device.

v0:
```python
import jax
import jax.numpy as jnp
from jax import lax
from jax.sharding import PartitionSpec as P


def shards(gate_input, up_input, code_values, exponents, cotangent):
    local_units = code_values.shape[0]
    scaled = jnp.exp2(exponents.astype(jnp.float32))
    blocks = code_values.astype(jnp.float32).reshape(local_units // 32, 32, -1) * scaled[:, None, :]
    weight_part = blocks.reshape(local_units, -1).astype(jnp.bfloat16)
    weight = lax.all_gather(weight_part, "depth", axis=1, tiled=True)
    gate_float = gate_input.astype(jnp.float32)
    up_float = up_input.astype(jnp.float32)
    sigmoid_gate = jax.nn.sigmoid(gate_float)
    activated = gate_float * sigmoid_gate
    hidden = (activated * up_float).astype(jnp.bfloat16)
    summed = lax.psum_scatter(
        lax.dot_general(
            weight, hidden, (((0,), (1,)), ((), ())), preferred_element_type=jnp.float32
        ),
        "grid",
        scatter_dimension=0,
        tiled=True,
    )
    output_rows = summed.T.astype(jnp.bfloat16)
    cotangent_all = lax.all_gather(cotangent, "grid", axis=1, tiled=True)
    grad_hidden = lax.dot_general(
        cotangent_all, weight, (((1,), (1,)), ((), ())), preferred_element_type=jnp.float32
    )
    slope = sigmoid_gate * (1.0 + gate_float * (1.0 - sigmoid_gate))
    grad_gate = (grad_hidden * up_float * slope).astype(jnp.bfloat16)
    grad_up = (grad_hidden * activated).astype(jnp.bfloat16)
    weight_term = lax.dot_general(
        hidden, cotangent_all, (((0,), (0,)), ((), ())), preferred_element_type=jnp.float32
    )
    grad_weight = lax.psum_scatter(weight_term, "depth", scatter_dimension=1, tiled=True).astype(
        jnp.bfloat16
    )
    return (output_rows, grad_gate, grad_up, grad_weight)


def solution(mesh):
    in_specs = (
        P(("parts", "depth"), "grid"),
        P(("parts", "depth"), "grid"),
        P("grid", "depth"),
        P("grid", "depth"),
        P(("parts", "depth"), "grid"),
    )
    out_specs = (
        P(("parts", "depth"), "grid"),
        P(("parts", "depth"), "grid"),
        P(("parts", "depth"), "grid"),
        P(("parts", "grid"), "depth"),
    )
    return jax.shard_map(shards, mesh=mesh, in_specs=in_specs, out_specs=out_specs, check_vma=False)
```

profile of v0, /device:TPU:0, one launch (start us, length us, event | category | flops | bytes accessed | tf_op | source)
XLA Modules:
  0.0 557.2 jit_solution(14383094031951518844)
XLA Ops:
  7.2 0.0 all-gather.3.cloned.1.call-start
  7.2 1.9 multiply_exponential_fusion
  9.1 23.3 %fusion = bf16[4096,4096]{1,0:T(8,128)(2,1)} fusion(bf16[4096,4096]{1,0:T(8,128)(2,1)} %param.7, f32[128,4096]{1,0:T(8,128)S(1)} %multiply_exponential_fusion), kind=kLoop, calls=%fused_computation.1 | loop fusion | flops 50331648 | bytes 69206016 | tf_op jit(solution)/shard_map/convert_element_type | solution.py:11
  32.3 0.0 all-gather.3.cloned.1.call-update
  32.4 0.0 all-gather.5.cloned.1.call-start
  32.4 0.7 all-gather.5.cloned.1.call-update
  33.1 0.0 reduce-scatter.3.cloned.1.call-start
  33.2 3.3 copy.9
  36.5 4.1 copy.10
  40.5 89.8 %all-gather.3.cloned.1.call-done = bf16[4096,8192]{1,0:T(8,128)(2,1)} async-done(((bf16[4096,4096]{1,0:T(8,128)(2,1)}), bf16[4096,8192]{1,0:T(8,128)(2,1)}) %all-gather.3.cloned.1.call-update) | async-done | bytes 67108880 | tf_op jit(solution)/shard_map/all_gather | solution.py:12
  130.3 30.2 %fusion.11 = f32[8192,256]{1,0:T(8,128)} fusion(bf16[4096,8192]{1,0:T(8,128)(2,1)} %all-gather.3.cloned.1.call-done, bf16[256,4096]{0,1:T(8,128)(2,1)} %copy.10, bf16[256,4096]{0,1:T(8,128)(2,1)S(1)} %copy.9), kind=kOutput, calls=%fused_computation.20 | convolution fusion | flops 17188257792 | bytes 79691776 | tf_op jit(solution)/shard_map/dot_general | solution.py:19
  160.5 0.0 reduce-scatter.3.cloned.1.call-update
  160.5 0.2 reduce-scatter.5.cloned.1.call-start
  160.8 46.3 %all-gather.5.cloned.1.call-done = bf16[256,8192]{1,0:T(8,128)(2,1)} async-done(((bf16[256,1024]{1,0:T(8,128)(2,1)}), bf16[256,8192]{1,0:T(8,128)(2,1)}) %all-gather.5.cloned.1.call-update) | async-done | bytes 4194320 | tf_op jit(solution)/shard_map/all_gather | solution.py:27
  207.1 49.9 %fusion.9 = f32[4096,8192]{1,0:T(8,128)} fusion(bf16[256,8192]{1,0:T(8,128)(2,1)} %all-gather.5.cloned.1.call-done, bf16[256,4096]{0,1:T(8,128)(2,1)} %copy.10, bf16[256,4096]{0,1:T(8,128)(2,1)S(1)} %copy.9), kind=kOutput, calls=%fused_computation.19 | convolution fusion | flops 17188257792 | bytes 142606336 | tf_op jit(solution)/shard_map/dot_general | solution.py:34
  257.0 0.0 reduce-scatter.5.cloned.1.call-update
  257.1 29.7 %multiply_convert_fusion = (bf16[256,4096]{0,1:T(8,128)(2,1)}, bf16[256,4096]{0,1:T(8,128)(2,1)}) fusion(bf16[256,4096]{0,1:T(8,128)(2,1)S(1)} %copy.9, bf16[256,4096]{0,1:T(8,128)(2,1)} %copy.10, bf16[4096,8192]{1,0:T(8,128)(2,1)} %all-gather.3.cloned.1.call-done, bf16[256,8192]{1,0:T(8,128)(2,1)} %all-gather.5.cloned.1.call-done), kind=kOutput, calls=%fused_computation.16 | convolution fusion | flops 17195597824 | bytes 79691776 | tf_op jit(solution)/shard_map/dot_general | solution.py:28
  286.7 0.0 copy-start
  286.7 4.3 copy.13
  291.0 0.0 copy-done
  291.0 2.8 copy.12
  293.9 64.7 %reduce-scatter.3.cloned.1.call-done = f32[1024,256]{1,0:T(8,128)} async-done(((f32[8192,256]{1,0:T(8,128)}), f32[1024,256]{1,0:T(8,128)}) %reduce-scatter.3.cloned.1.call-update) | async-done | bytes 1048592 | tf_op jit(solution)/shard_map/reduce_scatter | solution.py:18
  358.6 1.3 convert_bitcast_fusion
  359.8 1.0 copy.11
  360.8 157.4 %reduce-scatter.5.cloned.1.call-done = f32[4096,4096]{1,0:T(8,128)} async-done(((f32[4096,8192]{1,0:T(8,128)}), f32[4096,4096]{1,0:T(8,128)}) %reduce-scatter.5.cloned.1.call-update) | async-done | bytes 67108880 | tf_op jit(solution)/shard_map/reduce_scatter | solution.py:37
  518.3 32.4 %convert_element_type.43 = bf16[4096,4096]{1,0:T(8,128)(2,1)} convert(f32[4096,4096]{1,0:T(8,128)} %reduce-scatter.5.cloned.1.call-done) | non-fusion elementwise | flops 16777216 | bytes 100663296 | tf_op jit(solution)/shard_map/convert_element_type | solution.py:37
Async XLA Ops:
  7.2 123.2 %all-gather.3.cloned.1.call-start = ((), (), s32[]{:S(2)}) async-start(), calls=%async_computation.2 | async-start | bytes 100663296 | tf_op jit(solution)/shard_map/all_gather | solution.py:12
  32.4 174.7 %all-gather.5.cloned.1.call-start = ((), (), s32[]{:S(2)}) async-start(), calls=%async_computation.4 | async-start | bytes 4718592 | tf_op jit(solution)/shard_map/all_gather | solution.py:27
  33.1 325.4 %reduce-scatter.3.cloned.1.call-start = ((), (), s32[]{:S(2)}) async-start(), calls=%async_computation.3 | async-start | bytes 9437184 | tf_op jit(solution)/shard_map/reduce_scatter | solution.py:18
  160.5 357.7 %reduce-scatter.5.cloned.1.call-start = ((), (), s32[]{:S(2)}) async-start(), calls=%async_computation.5 | async-start | bytes 201326592 | tf_op jit(solution)/shard_map/reduce_scatter | solution.py:37
  286.7 4.3 copy-start
Sparse Core Ops, SparseCore 0:
  32.5 97.7 all-gather.2
  132.5 74.5 all-gather.4
  211.3 147.2 reduce-scatter.2
  360.8 157.4 reduce-scatter.4
where the time goes:
time: 558 us; the launch traced here: 557 us
  waiting for transfers between devices  359 us (64%)
  matrix products  110 us (20%)
  other arithmetic  58.8 us (11%)
  local copies, waits for them, and re-layouts  15.5 us (3%)
  between operations  13.8 us (2%)
    reduce_scatter x1, waiting for transfers between devices, shards(): lax.psum_scatter(weight_term, 'depth', scatter_dimension=1, tiled=True)  157 us
    all_gather x1, waiting for transfers between devices, shards(): weight = lax.all_gather(weight_part, 'depth', axis=1, tiled=True)  89.8 us
    reduce_scatter x1, waiting for transfers between devices, shards(): lax.psum_scatter(lax.dot_general(weight, hidden, (((0,), (1,)), ((), ()))...  64.7 us
    dot_general x1, matrix products, shards(): lax.dot_general(hidden, cotangent_all, (((0,), (0,)), ((), ())), preferre...  49.9 us
    all_gather x1, waiting for transfers between devices, shards(): cotangent_all = lax.all_gather(cotangent, 'grid', axis=1, tiled=True)  46.3 us
    convert_element_type x1, other arithmetic, shards(): lax.psum_scatter(weight_term, 'depth', scatter_dimension=1, tiled=True)  32.4 us
    dot_general x1, matrix products, shards(): lax.dot_general(weight, hidden, (((0,), (1,)), ((), ())), preferred_eleme...  30.2 us
    dot_general x1, matrix products, shards(): lax.dot_general(cotangent_all, weight, (((1,), (1,)), ((), ())), preferre...  29.7 us
  transfers between devices with their start and end apart: 4, of which 4 were waited for; matrix products, arithmetic and copies ran while one was open for 23% of the time, Pallas kernels for 0%

commit v1 on v0

--- a/solution.py
+++ b/solution.py
@@ -2,6 +2,25 @@
 import jax.numpy as jnp
 from jax import lax
 from jax.sharding import PartitionSpec as P
+
+
+def in_order(blocks, dim):
+    shape = list(blocks.shape[1:])
+    shape[dim] *= blocks.shape[0]
+    return jnp.moveaxis(blocks, 0, dim).reshape(shape)
+
+
+def collected_by_bits(value, axis):
+    length, index = (lax.axis_size(axis), lax.axis_index(axis))
+    blocks, bit = (value[None], 1)
+    while bit < length:
+        received = lax.ppermute(blocks, axis, [(i, i ^ bit) for i in range(length)])
+        low = index & bit == 0
+        blocks = jnp.concatenate(
+            [jnp.where(low, blocks, received), jnp.where(low, received, blocks)]
+        )
+        bit *= 2
+    return blocks
 
 
 def shards(gate_input, up_input, code_values, exponents, cotangent):
@@ -24,7 +43,7 @@
         tiled=True,
     )
     output_rows = summed.T.astype(jnp.bfloat16)
-    cotangent_all = lax.all_gather(cotangent, "grid", axis=1, tiled=True)
+    cotangent_all = in_order(collected_by_bits(cotangent, "grid"), 1)
     grad_hidden = lax.dot_general(
         cotangent_all, weight, (((1,), (1,)), ((), ())), preferred_element_type=jnp.float32
     )

time: 558 us -> 636 us (1.14)
  waiting for transfers between devices: 359 us -> 430 us
  local copies, waits for them, and re-layouts: 15.5 us -> 2 us
  matrix products: 110 us -> 120 us
  other arithmetic: 58.8 us -> 66.2 us
    ppermute x0 -> x3, waiting for transfers between devices: none -> 217 us  [collected_by_bits(): received = lax.ppermute(blocks, axis, [(i, i ^ bit) for i in range(length)])]
    reduce_scatter x1, waiting for transfers between devices: 64.7 us -> 0.01 us  [shards(): lax.psum_scatter(lax.dot_general(weight, hidden, (((0,), (1,)), ((), ()))...]
    all_gather x1 -> x0, waiting for transfers between devices: 46.3 us -> none  [shards(): cotangent_all = lax.all_gather(cotangent, 'grid', axis=1, tiled=True)]
    reduce_scatter x1, waiting for transfers between devices: 157 us -> 115 us  [shards(): lax.psum_scatter(weight_term, 'depth', scatter_dimension=1, tiled=True)]
    unnamed x7 -> x8, local copies, waits for them, and re-layouts: 15.5 us -> 2 us
    dot_general x1, matrix products: 29.7 us -> 41 us  [shards(): lax.dot_general(cotangent_all, weight, (((1,), (1,)), ((), ())), preferre...]
    all_gather x1, waiting for transfers between devices: 89.8 us -> 97.9 us  [shards(): weight = lax.all_gather(weight_part, 'depth', axis=1, tiled=True)]
  transfers between devices with their start and end apart: 4 -> 6, of which waited for: 4 -> 5; matrix products, arithmetic and copies ran while one was open for 23% -> 16% of each run, Pallas kernels for 0% -> 0%
where the time goes in v1:
time: 636 us
  waiting for transfers between devices  430 us (68%)
  matrix products  120 us (19%)
  other arithmetic  66.2 us (10%)
  between operations  13.8 us (2%)
    ppermute x3, waiting for transfers between devices, collected_by_bits(): received = lax.ppermute(blocks, axis, [(i, i ^ bit) for i in range(length)])  217 us
    reduce_scatter x1, waiting for transfers between devices, shards(): lax.psum_scatter(weight_term, 'depth', scatter_dimension=1, tiled=True)  115 us
    all_gather x1, waiting for transfers between devices, shards(): weight = lax.all_gather(weight_part, 'depth', axis=1, tiled=True)  97.9 us
    dot_general x1, matrix products, shards(): lax.dot_general(hidden, cotangent_all, (((0,), (0,)), ((), ())), preferre...  48.7 us
    dot_general x1, matrix products, shards(): lax.dot_general(cotangent_all, weight, (((1,), (1,)), ((), ())), preferre...  41 us
    convert_element_type x1, other arithmetic, shards(): lax.psum_scatter(weight_term, 'depth', scatter_dimension=1, tiled=True)  32.4 us
    dot_general x1, matrix products, shards(): lax.dot_general(weight, hidden, (((0,), (1,)), ((), ())), preferred_eleme...  30.4 us
    convert_element_type x1, other arithmetic, shards(): weight_part = blocks.reshape(local_units, -1).astype(jnp.bfloat16)  23.3 us
  transfers between devices with their start and end apart: 6, of which 5 were waited for; matrix products, arithmetic and copies ran while one was open for 16% of the time, Pallas kernels for 0%

profile of v1, /device:TPU:0, one launch (start us, length us, event | category | flops | bytes accessed | tf_op | source)
XLA Modules:
  0.0 635.5 jit_solution(11364330595222417558)
XLA Ops:
  7.2 0.0 all-gather.2.cloned.1.call-start
  7.2 1.9 multiply_exponential_fusion
  9.1 23.3 %fusion = bf16[4096,4096]{1,0:T(8,128)(2,1)} fusion(bf16[4096,4096]{1,0:T(8,128)(2,1)} %param.7, f32[128,4096]{1,0:T(8,128)S(1)} %multiply_exponential_fusion), kind=kLoop, calls=%fused_computation.1 | loop fusion | flops 50331648 | bytes 69206016 | tf_op jit(solution)/shard_map/convert_element_type | solution.py:30
  32.3 0.0 copy-start
  32.4 0.0 all-gather.2.cloned.1.call-update
  32.4 0.0 reduce-scatter.3.cloned.1.call-start
  32.4 97.9 %all-gather.2.cloned.1.call-done = bf16[4096,8192]{1,0:T(8,128)(2,1)} async-done(((bf16[4096,4096]{1,0:T(8,128)(2,1)}), bf16[4096,8192]{1,0:T(8,128)(2,1)}) %all-gather.2.cloned.1.call-update) | async-done | bytes 67108880 | tf_op jit(solution)/shard_map/all_gather | solution.py:31
  130.3 0.0 copy-done
  130.3 30.4 %fusion.11 = f32[8192,256]{1,0:T(8,128)} fusion(bf16[4096,8192]{1,0:T(8,128)(2,1)} %all-gather.2.cloned.1.call-done, bf16[256,4096]{1,0:T(8,128)(2,1)S(1)} %copy-done, bf16[256,4096]{1,0:T(8,128)(2,1)} %param.5), kind=kOutput, calls=%fused_computation.28 | convolution fusion | flops 17188257792 | bytes 79691776 | tf_op jit(solution)/shard_map/dot_general | solution.py:38
  160.7 0.0 copy-start.2
  160.7 0.0 reduce-scatter.3.cloned.1.call-update
  160.7 0.2 reduce-scatter.5.cloned.1.call-start
  161.0 0.8 copy-done.2
  161.8 0.2 copy.10
  162.0 1.8 collective-permute-start
  163.8 18.5 %collective-permute-done = bf16[1,256,1024]{1,2,0:T(8,128)(2,1)S(1)} collective-permute-done((bf16[1,256,1024]{1,2,0:T(8,128)(2,1)S(1)}, bf16[1,256,1024]{1,2,0:T(8,128)(2,1)S(1)}, u32[]{:S(2)}, u32[]{:S(2)}) %collective-permute-start) | collective-permute-done | bytes 524320 | tf_op jit(solution)/shard_map/ppermute | solution.py:17
  182.3 0.1 broadcast_select_fusion.5
  182.3 0.1 pad_maximum_fusion.2
  182.4 1.4 collective-permute-start.1
  183.9 72.0 %collective-permute-done.1 = bf16[2,256,1024]{1,2,0:T(8,128)(2,1)} collective-permute-done((bf16[2,256,1024]{1,2,0:T(8,128)(2,1)S(1)}, bf16[2,256,1024]{1,2,0:T(8,128)(2,1)}, u32[]{:S(2)}, u32[]{:S(2)}) %collective-permute-start.1) | collective-permute-done | bytes 1048608 | tf_op jit(solution)/shard_map/ppermute | solution.py:17
  255.8 1.4 broadcast_select_fusion.3
  257.2 1.5 pad_maximum_fusion.1
  258.7 0.0 collective-permute-start.2
  258.7 126.3 %collective-permute-done.2 = bf16[4,256,1024]{1,2,0:T(8,128)(2,1)} collective-permute-done((bf16[4,256,1024]{1,2,0:T(8,128)(2,1)}, bf16[4,256,1024]{1,2,0:T(8,128)(2,1)}, u32[]{:S(2)}, u32[]{:S(2)}) %collective-permute-start.2) | collective-permute-done | bytes 2097184 | tf_op jit(solution)/shard_map/ppermute | solution.py:17
  385.0 1.9 broadcast_select_fusion.1
  386.9 0.0 copy-start.1
  386.9 2.3 pad_maximum_fusion
  389.2 0.0 copy-done.1
  389.2 48.7 %fusion.9 = f32[4096,8192]{1,0:T(8,128)} fusion(bf16[256,8192]{0,1:T(8,128)(2,1)} %bitcast.17, bf16[256,4096]{1,0:T(8,128)(2,1)S(1)} %copy-done.1, bf16[256,4096]{1,0:T(8,128)(2,1)} %param.5), kind=kOutput, calls=%fused_computation.27 | convolution fusion | flops 17188257792 | bytes 142606336 | tf_op jit(solution)/shard_map/dot_general | solution.py:53
  437.9 0.0 reduce-scatter.5.cloned.1.call-update
  438.0 41.0 %multiply_convert_fusion = (bf16[256,4096]{1,0:T(8,128)(2,1)}, bf16[256,4096]{1,0:T(8,128)(2,1)}) fusion(bf16[256,4096]{1,0:T(8,128)(2,1)} %param.5, bf16[256,4096]{1,0:T(8,128)(2,1)S(1)} %copy-done.1, bf16[256,8192]{0,1:T(8,128)(2,1)} %bitcast.18, bf16[4096,8192]{1,0:T(8,128)(2,1)} %all-gather.2.cloned.1.call-done), kind=kOutput, calls=%fused_computation.16 | convolution fusion | flops 17195597824 | bytes 79691776 | tf_op jit(solution)/shard_map/dot_general | solution.py:47
  479.0 0.0 reduce-scatter.3.cloned.1.call-done
  479.0 1.5 convert_bitcast_fusion
  480.5 1.0 copy.11
  481.5 115.1 %reduce-scatter.5.cloned.1.call-done = f32[4096,4096]{1,0:T(8,128)} async-done(((f32[4096,8192]{1,0:T(8,128)}), f32[4096,4096]{1,0:T(8,128)}) %reduce-scatter.5.cloned.1.call-update) | async-done | bytes 67108880 | tf_op jit(solution)/shard_map/reduce_scatter | solution.py:56
  596.6 32.4 %convert_element_type.43 = bf16[4096,4096]{1,0:T(8,128)(2,1)} convert(f32[4096,4096]{1,0:T(8,128)} %reduce-scatter.5.cloned.1.call-done) | non-fusion elementwise | flops 16777216 | bytes 100663296 | tf_op jit(solution)/shard_map/convert_element_type | solution.py:56
Async XLA Ops:
  7.2 123.2 %all-gather.2.cloned.1.call-start = ((), (), s32[]{:S(2)}) async-start(), calls=%async_computation.2 | async-start | bytes 100663296 | tf_op jit(solution)/shard_map/all_gather | solution.py:31
  32.3 98.0 %copy-start = (bf16[256,4096]{1,0:T(8,128)(2,1)S(1)}, bf16[256,4096]{1,0:T(8,128)(2,1)}, u32[]{:S(2)}) copy-start(bf16[256,4096]{1,0:T(8,128)(2,1)} %param.6) | copy-start | bytes 6291460
  32.4 446.6 %reduce-scatter.3.cloned.1.call-start = ((), (), s32[]{:S(2)}) async-start(), calls=%async_computation.3 | async-start | bytes 9437184 | tf_op jit(solution)/shard_map/reduce_scatter | solution.py:37
  160.7 1.0 copy-start.2
  160.7 435.9 %reduce-scatter.5.cloned.1.call-start = ((), (), s32[]{:S(2)}) async-start(), calls=%async_computation.4 | async-start | bytes 201326592 | tf_op jit(solution)/shard_map/reduce_scatter | solution.py:56
  162.0 20.3 %collective-permute-start = (bf16[1,256,1024]{1,2,0:T(8,128)(2,1)S(1)}, bf16[1,256,1024]{1,2,0:T(8,128)(2,1)S(1)}, u32[]{:S(2)}, u32[]{:S(2)}) collective-permute-start(bf16[1,256,1024]{1,2,0:T(8,128)(2,1)S(1)} %bitcast.19), channel_id=1, source_target_pairs={{0,2},{2,0},{4,6},{6,4},{8,10},{10,8},{12,14},{14,12},{1,3},{3,1},... | collective-permute-start | bytes 1572872 | tf_op jit(solution)/shard_map/ppermute | solution.py:17
  182.4 73.4 %collective-permute-start.1 = (bf16[2,256,1024]{1,2,0:T(8,128)(2,1)S(1)}, bf16[2,256,1024]{1,2,0:T(8,128)(2,1)}, u32[]{:S(2)}, u32[]{:S(2)}) collective-permute-start(bf16[2,256,1024]{1,2,0:T(8,128)(2,1)S(1)} %pad_maximum_fusion.2), channel_id=1, source_target_pairs={{0,4},{2,6},{4,0},{6,2},{8,12},{10,14},{12,8},{14,10},{1,5},{3,7},... | collective-permute-start | bytes 3145736 | tf_op jit(solution)/shard_map/ppermute | solution.py:17
  258.7 126.3 %collective-permute-start.2 = (bf16[4,256,1024]{1,2,0:T(8,128)(2,1)}, bf16[4,256,1024]{1,2,0:T(8,128)(2,1)}, u32[]{:S(2)}, u32[]{:S(2)}) collective-permute-start(bf16[4,256,1024]{1,2,0:T(8,128)(2,1)} %pad_maximum_fusion.1), channel_id=1, source_target_pairs={{0,8},{2,10},{4,12},{6,14},{8,0},{10,2},{12,4},{14,6},{1,9},{3,11}... | collective-permute-start | bytes 6291464 | tf_op jit(solution)/shard_map/ppermute | solution.py:17
  386.9 2.3 copy-start.1
Sparse Core Ops, SparseCore 0:
  32.5 97.7 all-gather.1
  160.9 199.2 reduce-scatter.2
  438.1 158.5 reduce-scatter.4
